TPU v7x, 32 devices: a whole 2x2x4 slice. The times are simulated.
32 devices in a mesh: groups: 2 (over y), tmpl: 4 (over z), region: 2 (over x), sub: 2 (over core).
Axes of the slice: x: 2, y: 2, z: 4, core: 2. Of those that a mesh axis runs over, the one named last changes fastest.
Arguments:
- waveforms: float32 [2, 16, 4096], P('region', ('tmpl', 'sub'), 'groups'), parts along dimension 2
- templates: bfloat16 [2, 192, 12, 400], P('region', ('tmpl', 'sub'))
- channel_ids: int32 [2, 192, 12], P('region', ('tmpl', 'sub')), may hold values from 0 to 31, as said below
- moveouts: int32 [2, 192, 12], P('region', ('tmpl', 'sub')), may hold values from 0 to 511
- active: int32 [2, 192], P('region', ('tmpl', 'sub')), may hold values from 6 to 12
- border: int32 [2, 2, 8], P('region'), may hold values from 0 to 15, as said below
- border_count: int32 [2, 2], P('region'), may hold values from 1 to 8
Outputs:
- scores: float32 [2, 192, 1024], P('region', ('tmpl', 'sub'), 'groups'), parts along dimension 2
There are 2 independent parts, one for each index of `groups`. A program takes and returns all parts, laid end to end along the dimension named above; an argument that names none is the same for every part. Nothing has to cross between parts.
Inputs may be any that keep to these rules, and one draw needn't show every extreme that they name: `channel_ids`: the 12 entries of a template are distinct. An entry below 16 is one of the region's own channels; 16 + i is entry i of the previous region's side 1 border list and 24 + i entry i of the next region's side 0 border list; such an entry appears only where that region exists and i is below that list's border_count. `border`: each list names 8 distinct channels of its region.
All inputs are finite; a program needn't handle non-finite values.
Results may differ from a plain program's by a relative error of at most 0.0081.
Values sent between devices are 32-bit elements; how exact they have to be, the bound alone decides.
A program may use at most 64 MiB of HBM per device.

v0:
```python
import math

import jax
import jax.numpy as jnp
from jax import lax
from jax.sharding import PartitionSpec as P

NF = 2048
F0 = 40
BAND = 384
K = 400
SLOTS = 12
OUT = 512
LN = 1024


EPSILON = 1e-06


def shifted(block, axis, distance):
    devices = range(lax.axis_size(axis))
    route = [(i - distance, i) for i in devices if i - distance in devices]
    return lax.ppermute(block, axis, route)


def angles(samples, first_bin, bins, length):
    sample_ids = jnp.arange(samples, dtype=jnp.int32)[:, None]
    bin_ids = first_bin + jnp.arange(bins, dtype=jnp.int32)[None, :]
    turn_count = sample_ids * bin_ids % length
    return turn_count.astype(jnp.float32) * (2.0 * math.pi / length)


def forward_table(samples, first_bin, bins, length):
    phases = angles(samples, first_bin, bins, length)
    return jnp.concatenate([jnp.cos(phases), -jnp.sin(phases)], axis=1)


def inverse_table(samples, first_bin, bins, length):
    phases = jnp.transpose(angles(samples, first_bin, bins, length))
    return jnp.concatenate([jnp.cos(phases), -jnp.sin(phases)], axis=0)


def slide_sum(filtered):
    running = jnp.cumsum(filtered * filtered, axis=1)
    running = jnp.concatenate([jnp.zeros((running.shape[0], 1), jnp.float32), running], axis=1)
    return running[:, K : K + LN] - running[:, :LN]


def window_energy(spectra):
    lag_rows = inverse_table(NF, F0, BAND, NF)
    filtered = (
        2.0
        / NF
        * jnp.dot(
            spectra, lag_rows, precision=lax.Precision.HIGHEST, preferred_element_type=jnp.float32
        )
    )
    return slide_sum(filtered)


def pick_rows(payload, indices, live_count):
    chosen = jnp.take(payload, indices, axis=0)
    places = jnp.arange(indices.shape[0], dtype=jnp.int32)
    return jnp.where((places < live_count)[:, None], chosen, jnp.zeros_like(chosen))


def cross_spectrum(tmpl_spectra, data_spectra):
    half_bins = tmpl_spectra.shape[1] // 2
    tmpl_real = tmpl_spectra[:, :half_bins]
    tmpl_imag = tmpl_spectra[:, half_bins:]
    data_real = data_spectra[:, :half_bins]
    data_imag = data_spectra[:, half_bins:]
    return jnp.concatenate(
        [
            tmpl_real * data_real + tmpl_imag * data_imag,
            tmpl_real * data_imag - tmpl_imag * data_real,
        ],
        axis=1,
    )


def block_scores(block_items, ext_spectra, station_norm, short_table, lag_table):
    block_waves, block_ids, block_moves, block_active = block_items
    templ_count = block_waves.shape[0]
    slot_count = block_waves.shape[1]
    flat_waves = block_waves.reshape(templ_count * slot_count, block_waves.shape[2])
    tmpl_spectra = jnp.dot(flat_waves, short_table, preferred_element_type=jnp.float32)
    tmpl_norm = jnp.sqrt(jnp.sum(jnp.square(flat_waves.astype(jnp.float32)), axis=1) + EPSILON)
    flat_ids = block_ids.reshape(-1)
    cross_terms = cross_spectrum(tmpl_spectra, jnp.take(ext_spectra, flat_ids, axis=0)).astype(
        jnp.bfloat16
    )
    correlation = 2.0 / NF * jnp.dot(cross_terms, lag_table, preferred_element_type=jnp.float32)
    normed = correlation / (tmpl_norm[:, None] * jnp.take(station_norm, flat_ids, axis=0))
    aligned = jax.vmap(lambda series, offset: lax.dynamic_slice_in_dim(series, offset, OUT))(
        normed, block_moves.reshape(-1)
    )
    weights = (jnp.arange(slot_count, dtype=jnp.int32)[None, :] < block_active[:, None]).astype(
        jnp.float32
    )
    return jnp.sum(aligned.reshape(templ_count, slot_count, OUT) * weights[:, :, None], axis=1)


def on_device(waveforms, templates, channel_ids, moveouts, active, border, border_count):
    own_spectra = jnp.dot(
        waveforms[0],
        forward_table(NF, F0, BAND, NF),
        precision=lax.Precision.HIGHEST,
        preferred_element_type=jnp.float32,
    )
    payload = jnp.concatenate([own_spectra, window_energy(own_spectra)], axis=1)
    region_rows = lax.all_gather(payload, ("tmpl", "sub"), axis=0, tiled=True)
    border_lists = border[0]
    border_sizes = border_count[0]
    right_rows = pick_rows(region_rows, border_lists[1], border_sizes[1])
    left_rows = pick_rows(region_rows, border_lists[0], border_sizes[0])
    from_left = shifted(right_rows, "region", 1)
    from_right = shifted(left_rows, "region", -1)
    extended = jnp.concatenate([region_rows, from_left, from_right], axis=0)
    ext_spectra = extended[:, : 2 * BAND]
    ext_energy = extended[:, 2 * BAND :]
    station_norm = jnp.sqrt(ext_energy + EPSILON)
    short_table = forward_table(K, F0, BAND, NF).astype(jnp.bfloat16)
    lag_table = inverse_table(LN, F0, BAND, NF).astype(jnp.bfloat16)
    local_waves = templates[0]
    templ_total = local_waves.shape[0]
    block_total = templ_total // templ_total

    def run_block(block_items):
        return block_scores(block_items, ext_spectra, station_norm, short_table, lag_table)

    stacked = lax.map(
        run_block,
        (
            local_waves.reshape(block_total, templ_total, SLOTS, K),
            channel_ids[0].reshape(block_total, templ_total, SLOTS),
            moveouts[0].reshape(block_total, templ_total, SLOTS),
            active[0].reshape(block_total, templ_total),
        ),
    )
    return stacked


def solution(mesh):
    in_specs = (
        P("region", ("tmpl", "sub"), "groups"),
        P("region", ("tmpl", "sub"), None, None),
        P("region", ("tmpl", "sub"), None),
        P("region", ("tmpl", "sub"), None),
        P("region", ("tmpl", "sub")),
        P("region", None, None),
        P("region", None),
    )
    out_specs = P("region", ("tmpl", "sub"), "groups")
    return jax.shard_map(
        on_device, mesh=mesh, in_specs=in_specs, out_specs=out_specs, check_vma=False
    )
```

profile of v0, /device:TPU:0, one launch (start us, length us, event | category | flops | bytes accessed | tf_op | source)
XLA Modules:
  0.0 648.9 jit_solution(16783452596899692987)
XLA Ops:
  0.0 12.6 %fusion.36 = (f32[2048,384]{1,0:T(8,128)S(1)}, f32[2048,384]{1,0:T(8,128)S(1)}) fusion(s32[384]{0:T(512)S(1)} %iota_add_fusion), kind=kLoop, calls=%fused_computation.50 | loop fusion | flops 11796480 | bytes 6292992 | tf_op jit(solution)/shard_map/cos | solution.py:35
  12.6 12.7 %fusion.35 = (f32[384,2048]{1,0:T(8,128)S(1)}, f32[384,2048]{1,0:T(8,128)S(1)}) fusion(s32[384]{0:T(512)S(1)} %iota_add_fusion), kind=kLoop, calls=%fused_computation.49 | loop fusion | flops 11796480 | bytes 6292992 | tf_op jit(solution)/shard_map/cos | solution.py:40
  25.3 3.3 fusion
  28.7 3.1 fusion.41
  32.9 15.7 %all-gather = f32[8,2,1792]{2,1,0:T(2,128)S(1)} all-gather(f32[1,2,1792]{2,1,0:T(2,128)S(1)} %maximum_bitcast_fusion), channel_id=1, replica_groups=mesh['groups'=2,'tmpl'=4,'region'=2,'sub'=2] {'tmpl','sub'}, dimensions={0}, use_global_device_ids=true | all-gather | bytes 129024 | tf_op jit(solution)/shard_map/all_gather | solution.py:112
  50.6 3.4 collective-permute-start
  56.9 2.8 cosine_convert_fusion.1
  59.7 8.2 %cosine_convert_fusion = (bf16[384,1024]{1,0:T(8,128)(2,1)}, bf16[384,1024]{1,0:T(8,128)(2,1)}) fusion(s32[384]{0:T(512)S(1)} %iota_add_fusion), kind=kLoop, calls=%fused_computation.46 | loop fusion | flops 6684672 | bytes 1574400 | tf_op jit(solution)/shard_map/convert
  69.3 1.9 gather_fusion
  71.2 1.8 gather_fusion.1
  75.5 572.5 %while.1 = (s32[]{:T(128)}, f32[288,1024]{1,0:T(8,128)S(1)}, s32[288,2]{0,1:T(2,128)S(1)}, f32[288,512]{1,0:T(8,128)S(1)}, s32[]{:T(128)}, /*index=5*/s32[]{:T(128)}) while((s32[]{:T(128)}, f32[288,1024]{1,0:T(8,128)S(1)}, s32[288,2]{0,1:T(2,128)S(1)}, f32[288,512]{1,0:T(8,128)S(1)}, s32[]{:T(128)}, /*index=5*/s32[]{:T(128)}) %tuple.36), condition=%wide.while_cond, body=%wide.while_body.sunk | while | flops 2 | bytes 8305 | solution.py:95
  76.1 1.3 dynamic-slice.7
  80.1 1.3 dynamic-slice.7
  82.1 1.3 dynamic-slice.7
  88.0 1.3 dynamic-slice.7
  90.0 1.3 dynamic-slice.7
  96.0 1.3 dynamic-slice.7
  98.0 1.3 dynamic-slice.7
  103.9 1.3 dynamic-slice.7
  105.9 1.3 dynamic-slice.7
  109.9 1.3 dynamic-slice.7
  111.9 1.3 dynamic-slice.7
  113.9 1.3 dynamic-slice.7
  117.8 1.3 dynamic-slice.7
  (1212 shorter events, 559.2 us)
Async XLA Ops:
  0.0 25.3 %copy-start = (f32[1,2,2048]{2,1,0:T(2,128)S(1)}, f32[1,2,2048]{2,1,0:T(2,128)}, u32[]{:S(2)}) copy-start(f32[1,2,2048]{2,1,0:T(2,128)} %param.9) | copy-start | bytes 49156
  28.6 20.0 %copy-start.7 = (s32[1,2]{1,0:T(1,128)S(1)}, s32[1,2]{1,0:T(1,128)}, u32[]{:S(2)}) copy-start(s32[1,2]{1,0:T(1,128)} %param.15) | copy-start | bytes 28
  28.6 20.6 %copy-start.8 = (s32[1,2,8]{2,1,0:T(2,128)S(1)}, s32[1,2,8]{2,1,0:T(2,128)}, u32[]{:S(2)}) copy-start(s32[1,2,8]{2,1,0:T(2,128)} %param.14) | copy-start | bytes 196
  28.7 27.9 %copy-start.5 = (s32[1,24,12]{1,0,2:T(1,128)S(1)}, s32[1,24,12]{1,0,2:T(1,128)}, u32[]{:S(2)}) copy-start(s32[1,24,12]{1,0,2:T(1,128)} %param.11) | copy-start | bytes 3460
  31.7 36.1 %copy-start.1 = (bf16[1,24,12,400]{3,1,2,0:T(8,128)(2,1)S(1)}, bf16[1,24,12,400]{3,1,2,0:T(8,128)(2,1)}, u32[]{:S(2)}) copy-start(bf16[1,24,12,400]{3,1,2,0:T(8,128)(2,1)} %param.10) | copy-start | bytes 691204
  31.7 36.8 %copy-start.6 = (s32[1,24,12]{1,0,2:T(1,128)S(1)}, s32[1,24,12]{1,0,2:T(1,128)}, u32[]{:S(2)}) copy-start(s32[1,24,12]{1,0,2:T(1,128)} %param.12) | copy-start | bytes 3460
  31.7 37.0 %copy-start.9 = (s32[1,24]{1,0:T(1,128)S(1)}, s32[1,24]{1,0:T(1,128)}, u32[]{:S(2)}) copy-start(s32[1,24]{1,0:T(1,128)} %param.13) | copy-start | bytes 292
  50.6 18.7 %collective-permute-start = (f32[8,1792]{1,0:T(8,128)S(1)}, f32[8,1792]{1,0:T(8,128)S(1)}, u32[]{:S(2)}, u32[]{:S(2)}) collective-permute-start(f32[8,1792]{1,0:T(8,128)S(1)} %select_select_fusion.1), channel_id=1, source_target_pairs={{0,2},{1,3},{4,6},{5,7},{8,10},{9,11},{12,14},{13,15},{16,18},{17,... | collective-permute-start | bytes 172040 | tf_op jit(solution)/shard_map/ppermute | solution.py:23
  55.3 14.0 %collective-permute-start.1 = (f32[8,1792]{1,0:T(8,128)S(1)}, f32[8,1792]{1,0:T(8,128)S(1)}, u32[]{:S(2)}, u32[]{:S(2)}) collective-permute-start(f32[8,1792]{1,0:T(8,128)S(1)} %select_select_fusion), channel_id=1, source_target_pairs={{2,0},{3,1},{6,4},{7,5},{10,8},{11,9},{14,12},{15,13},{18,16},{19,... | collective-permute-start | bytes 172040 | tf_op jit(solution)/shard_map/ppermute | solution.py:23
  73.0 1.1 copy-start.2
  73.0 1.4 copy-start.3
  74.4 1.1 copy-start.4
where the time goes:
time: 654 us; the launch traced here: 649 us
  local copies, waits for them, and re-layouts  573 us (88%)
  other arithmetic  40.3 us (6%)
  blocking collectives  15.7 us (2%)
  matrix products  7.43 us (1%)
  loops' own time  6.96 us (1%)
    gather x1152, local copies, waits for them, and re-layouts  566 us
    all_gather x1, blocking collectives, on_device(): region_rows = lax.all_gather(payload, ('tmpl', 'sub'), axis=0, tiled=True)  15.7 us
  transfers between devices with their start and end apart: 2, of which 0 were waited for; matrix products, arithmetic and copies ran while one was open for 2% of the time, Pallas kernels for 0%

commit v1 on v0

v1 whole, which is shorter than its diff:
```python
import functools

import jax
import jax.numpy as jnp
import ml_dtypes
import numpy as np
from jax import lax
from jax.experimental import pallas as pl
from jax.experimental.pallas import tpu as pltpu
from jax.sharding import PartitionSpec as P

NF = 2048
F0 = 40
BAND = 384
K = 400
OUT = 512
LN = 1024
EPSILON = 1e-06

LANES = 128
RES = NF // LANES
STEPS = BAND // RES
CHUNKS = (2 * BAND + LN) // LANES
SPEC_CHUNKS = 2 * BAND // LANES
MESH = pl.DeviceIdType.MESH
HIGH = lax.Precision.HIGHEST


def dot(a, b):
    return jnp.dot(a, b, precision=HIGH, preferred_element_type=jnp.float32)


def bin_order():
    r, g = np.meshgrid(np.arange(RES), np.arange(STEPS), indexing="ij")
    return (F0 + RES * g + r).reshape(-1)


def wide_tables():
    bins = bin_order()
    turn = 2.0 * np.pi / NF
    short = (np.arange(K)[:, None] * bins[None, :] % NF) * turn
    short = np.concatenate([np.cos(short), -np.sin(short)], axis=1)
    lag = (bins[:, None] * np.arange(LN)[None, :] % NF) * turn
    lag = np.concatenate([np.cos(lag), -np.sin(lag)], axis=0)
    as_bf16 = lambda x: x.astype(np.float32).astype(ml_dtypes.bfloat16)
    return as_bf16(short), as_bf16(lag)


def small_tables(chans):
    turn = 2.0 * np.pi / NF
    r, a, b, g = np.arange(RES), np.arange(RES), np.arange(LANES), np.arange(STEPS)
    eye = np.eye(chans)
    alpha = (F0 + r)[:, None] * a[None, :] * LANES % NF * turn
    gather = np.concatenate([np.kron(np.cos(alpha), eye), np.kron(-np.sin(alpha), eye)], axis=0)
    spread = 2.0 / NF * np.concatenate(
        [np.kron(np.cos(alpha.T), eye), np.kron(-np.sin(alpha.T), eye)], axis=1
    )
    theta = np.repeat((F0 + r)[:, None] * b[None, :] % NF * turn, chans, axis=0)
    twiddle = np.concatenate([np.cos(theta), np.sin(theta)], axis=0)
    beta = b[:, None] * g[None, :] * RES % NF * turn
    c, s = np.cos(beta), np.sin(beta)
    fwd = np.zeros((2 * LANES, LANES))
    fwd[:LANES, :STEPS], fwd[:LANES, STEPS : 2 * STEPS] = c, -s
    fwd[LANES:, :STEPS], fwd[LANES:, STEPS : 2 * STEPS] = s, c
    inv = np.zeros((LANES, 2 * LANES))
    inv[:STEPS, :LANES], inv[:STEPS, LANES:] = c.T, s.T
    inv[STEPS : 2 * STEPS, :LANES], inv[STEPS : 2 * STEPS, LANES:] = -s.T, c.T
    rows = []
    for i in (0, 1, 3, 4):
        place = LANES * i + b[:, None] - b[None, :]
        rows.append((place >= 0) & (place < K))
    window = np.concatenate(rows, axis=0)
    return [x.astype(np.float32) for x in (gather, spread, twiddle, fwd, inv, window)]


def station_kernel(
    geometry, wave_ref, border_ref, count_ref, tmpl_ref, short_ref, gather_ref, spread_ref,
    twiddle_ref, fwd_ref, inv_ref, window_ref, recv_ref, tspec_ref, scale_ref,
    pay_ref, rows_ref, spec_ref, pad_ref, send_sem, recv_sem,
):
    regions, tmpls, subs, offsets = geometry
    group = tmpls * subs
    region = lax.axis_index("region")
    place = lax.axis_index("tmpl") * subs + lax.axis_index("sub")
    peers = []
    for block, offset in enumerate(offsets):
        there = lax.rem(region + (regions - offset) % regions, regions)
        for step in range(1 if offset == 0 else 0, group):
            peer = lax.rem(place + step, group)
            device = {"region": there, "tmpl": peer // subs, "sub": lax.rem(peer, subs)}
            peers.append((block, step, peer, device))
    barrier = pltpu.get_barrier_semaphore()
    for _, _, _, device in peers:
        pl.semaphore_signal(barrier, inc=1, device_id=device, device_id_type=MESH)

    chans = wave_ref.shape[0]
    half = RES * chans
    for a in range(RES):
        rows_ref[chans * a : chans * (a + 1), :] = wave_ref[:, LANES * a : LANES * (a + 1)]
    y = dot(gather_ref[...], rows_ref[...])
    cos, sin = twiddle_ref[:half, :], twiddle_ref[half:, :]
    yr, yi = y[:half], y[half:]
    z = jnp.concatenate([yr * cos + yi * sin, yi * cos - yr * sin], axis=1)
    x = dot(z, fwd_ref[...])
    for r in range(RES):
        piece = x[chans * r : chans * (r + 1), :]
        spec_ref[:, STEPS * r : STEPS * (r + 1)] = piece[:, :STEPS]
        spec_ref[:, BAND + STEPS * r : BAND + STEPS * (r + 1)] = piece[:, STEPS : 2 * STEPS]
    for k in range(SPEC_CHUNKS):
        pay_ref[chans * k : chans * (k + 1), :] = spec_ref[:, LANES * k : LANES * (k + 1)]
    v = dot(x, inv_ref[...])
    vr, vi = v[:, :LANES], v[:, LANES:]
    u = jnp.concatenate([vr * cos - vi * sin, vr * sin + vi * cos], axis=0)
    filtered = dot(spread_ref[...], u)
    rows_ref[...] = filtered * filtered
    count = LN // LANES * chans
    near = lambda i: rows_ref[chans * i : chans * i + count, :]
    pieces = jnp.concatenate([near(0), near(1) + near(2), near(3), near(4)], axis=1)
    start = chans * SPEC_CHUNKS
    pay_ref[start : start + count, :] = dot(pieces, window_ref[...])
    bmax = border_ref.shape[1]
    base = chans * CHUNKS
    pay_ref[base:, :] = jnp.zeros((pay_ref.shape[0] - base, LANES), jnp.float32)
    pay_ref[base : base + 1, :bmax] = border_ref[1:2, :].astype(jnp.float32)
    pay_ref[base + 1 : base + 2, :bmax] = border_ref[0:1, :].astype(jnp.float32)
    pay_ref[base + 2 : base + 3, :2] = count_ref[...].astype(jnp.float32)

    pl.semaphore_wait(barrier, len(peers))
    copies = []
    for block, step, peer, device in peers:
        copy = pltpu.make_async_remote_copy(
            src_ref=pay_ref,
            dst_ref=recv_ref.at[block * group + place],
            send_sem=send_sem.at[block * group + step],
            recv_sem=recv_sem.at[block * group + place],
            device_id=device,
            device_id_type=MESH,
        )
        copy.start()
        copies.append(copy)
    recv_ref[pl.ds(place, 1)] = pay_ref[...][None]

    templs, slots, _ = tmpl_ref.shape
    pad_ref[...] = jnp.zeros_like(pad_ref)
    for t in range(templs):
        pad_ref[t, :slots, :] = tmpl_ref[t]
    waves = pad_ref[...].reshape(templs * pad_ref.shape[1], K)
    tspec_ref[...] = jnp.dot(waves, short_ref[...], preferred_element_type=jnp.float32)
    wide = waves.astype(jnp.float32)
    power = jnp.sum(wide * wide, axis=1, keepdims=True)
    scale_ref[...] = 2.0 / NF * lax.rsqrt(power + EPSILON)

    for copy in copies:
        copy.wait_send()
    for block, step, peer, device in peers:
        slot = block * group + peer
        pltpu.make_async_remote_copy(
            src_ref=pay_ref,
            dst_ref=recv_ref.at[slot],
            send_sem=send_sem.at[block * group + step],
            recv_sem=recv_sem.at[slot],
            device_id=device,
            device_id_type=MESH,
        ).wait_recv()


def match_kernel(
    geometry, chans, bmax, recv_ref, tspec_ref, scale_ref, ids_ref, move_ref, active_ref, lag_ref,
    out_ref, table_ref, parts_ref, cross_ref, line_ref, sums_ref,
):
    regions, tmpls, subs, offsets = geometry
    group = tmpls * subs
    own = group * chans
    total = own * len(offsets)
    ext = own + 2 * bmax
    templs, slots = ids_ref.shape
    padded = tspec_ref.shape[0] // templs
    wide = padded * templs
    bf16, f32 = jnp.bfloat16, jnp.float32

    for d in range(group * len(offsets)):
        for k in range(CHUNKS):
            table_ref[chans * d : chans * (d + 1), LANES * k : LANES * (k + 1)] = recv_ref[
                d, chans * k : chans * (k + 1), :
            ]
    table_ref[:, 2 * BAND :] = lax.rsqrt(table_ref[:, 2 * BAND :] + EPSILON)
    table = table_ref[...]
    high = table.astype(bf16)
    rest = table - high.astype(f32)
    middle = rest.astype(bf16)
    low = (rest - middle.astype(f32)).astype(bf16)
    parts_ref[...] = jnp.concatenate([high, middle, low], axis=0)

    region = lax.axis_index("region")
    left = offsets.index((regions - 1) % regions)
    right = offsets.index(1 % regions)
    base = chans * CHUNKS
    lane = lax.broadcasted_iota(jnp.int32, (1, LANES), 1)
    info = recv_ref[left * group, base : base + 3, :]
    from_left = info[0:1].astype(jnp.int32)
    left_count = jnp.where(region > 0, info[2:3, 1:2].astype(jnp.int32), 0)
    info = recv_ref[right * group, base : base + 3, :]
    from_right = info[1:2].astype(jnp.int32)
    right_count = jnp.where(region < regions - 1, info[2:3, 0:1].astype(jnp.int32), 0)
    row = lax.broadcasted_iota(jnp.int32, (3 * total, 1), 0) % total
    one = lambda mask: jnp.where(mask, 1.0, 0.0).astype(bf16)
    own_pick = one(row == lane[:, :own])
    left_pick = one((row == left * own + from_left[:, :bmax]) & (lane[:, :bmax] < left_count))
    right_pick = one((row == right * own + from_right[:, :bmax]) & (lane[:, :bmax] < right_count))

    slot_row = lax.broadcasted_iota(jnp.int32, (wide, 1), 0)
    spread = one(slot_row // padded == lax.broadcasted_iota(jnp.int32, (wide, templs), 1))
    ids = ids_ref[...].astype(f32).astype(bf16)
    ids = jnp.dot(spread, ids, preferred_element_type=f32)
    mine = slot_row % padded == lax.broadcasted_iota(jnp.int32, (wide, slots), 1)
    ids = jnp.sum(jnp.where(mine, ids, 0.0), axis=1, keepdims=True).astype(jnp.int32)
    contract = (((1,), (1,)), ((), ()))
    pick = lambda first, rows_pick: lax.dot_general(
        one(ids == first + lane[:, : rows_pick.shape[1]]), rows_pick, contract,
        preferred_element_type=f32,
    )
    chosen = pick(0, own_pick) + pick(own, left_pick) + pick(own + bmax, right_pick)
    chosen = chosen.astype(bf16)

    spec = jnp.dot(chosen, parts_ref[:, : 2 * BAND], preferred_element_type=f32)
    xr, xi = spec[:, :BAND], spec[:, BAND:]
    wr, wi = tspec_ref[:, :BAND], tspec_ref[:, BAND:]
    cross_ref[:, :BAND] = (wr * xr + wi * xi).astype(bf16)
    cross_ref[:, BAND:] = (wr * xi - wi * xr).astype(bf16)
    unsent = (1.0 - jnp.sum(chosen.astype(f32), axis=1, keepdims=True) / 3.0) * EPSILON**-0.5
    step = 2 * LANES
    for c in range(0, LN, step):
        corr = jnp.dot(cross_ref[...], lag_ref[:, c : c + step], preferred_element_type=f32)
        inv = jnp.dot(
            chosen, parts_ref[:, 2 * BAND + c : 2 * BAND + c + step], preferred_element_type=f32
        )
        normed = corr * (inv + unsent) * scale_ref[...]
        for k in range(step // LANES):
            line_ref[pl.ds(c // LANES + k, wide, stride=LN // LANES), :] = normed[
                :, LANES * k : LANES * (k + 1)
            ]

    rows_out = OUT // LANES
    lane4 = lax.broadcasted_iota(jnp.int32, (rows_out, LANES), 1)

    def one_template(t, carry):
        total_score = jnp.zeros((rows_out, LANES), f32)
        used = active_ref[0, t]
        for j in range(slots):
            move = move_ref[t, j]
            q, s = move // LANES, move % LANES
            start = (t * padded + j) * (LN // LANES) + q
            first = line_ref[pl.ds(start, rows_out), :]
            second = line_ref[pl.ds(start + 1, rows_out), :]
            joined = jnp.where(lane4 >= s, first, second)
            turned = pltpu.roll(joined, (LANES - s) % LANES, 1)
            total_score += turned * jnp.where(j < used, 1.0, 0.0)
        sums_ref[pl.ds(t * rows_out, rows_out), :] = total_score
        return carry

    lax.fori_loop(0, templs, one_template, 0)
    for a in range(rows_out):
        out_ref[:, LANES * a : LANES * (a + 1)] = sums_ref[pl.ds(a, templs, stride=rows_out), :]


def on_device(
    geometry, waveforms, templates, channel_ids, moveouts, active, border, border_count
):
    regions, tmpls, subs, offsets = geometry
    devices = tmpls * subs * len(offsets)
    chans = waveforms.shape[1]
    bmax = border.shape[2]
    templs, slots = channel_ids.shape[1:]
    padded = -(-slots // 16) * 16
    wide = templs * padded
    short_table, lag_table = wide_tables()
    pay_rows = -(-(chans * CHUNKS + 3) // 8) * 8
    vmem = pl.BlockSpec(memory_space=pltpu.VMEM)
    smem = pl.BlockSpec(memory_space=pltpu.SMEM)
    f32, bf16 = jnp.float32, jnp.bfloat16
    recv, tspec, scale = pl.pallas_call(
        functools.partial(station_kernel, geometry),
        out_shape=(
            jax.ShapeDtypeStruct((devices, pay_rows, LANES), f32),
            jax.ShapeDtypeStruct((wide, 2 * BAND), f32),
            jax.ShapeDtypeStruct((wide, 1), f32),
        ),
        in_specs=[vmem] * 11,
        out_specs=(vmem, vmem, vmem),
        scratch_shapes=[
            pltpu.VMEM((pay_rows, LANES), f32),
            pltpu.VMEM((RES * chans, LANES), f32),
            pltpu.VMEM((chans, 2 * BAND), f32),
            pltpu.VMEM((templs, padded, K), bf16),
            pltpu.SemaphoreType.DMA((devices,)),
            pltpu.SemaphoreType.DMA((devices,)),
        ],
        compiler_params=pltpu.CompilerParams(collective_id=0, has_side_effects=True),
        name="stations",
    )(
        waveforms[0], border[0], border_count, templates[0], short_table,
        *small_tables(chans),
    )
    scores = pl.pallas_call(
        functools.partial(match_kernel, geometry, chans, bmax),
        out_shape=jax.ShapeDtypeStruct((templs, OUT), f32),
        in_specs=[vmem, vmem, vmem, vmem, smem, smem, vmem],
        out_specs=vmem,
        scratch_shapes=[
            pltpu.VMEM((chans * devices, CHUNKS * LANES), f32),
            pltpu.VMEM((3 * chans * devices, CHUNKS * LANES), bf16),
            pltpu.VMEM((wide, 2 * BAND), bf16),
            pltpu.VMEM((wide * (LN // LANES), LANES), f32),
            pltpu.VMEM((templs * (OUT // LANES), LANES), f32),
        ],
        name="match",
    )(recv, tspec, scale, channel_ids[0], moveouts[0], active, lag_table)
    return scores[None]


def solution(mesh):
    regions, tmpls, subs = (mesh.shape[a] for a in ("region", "tmpl", "sub"))
    offsets = tuple(dict.fromkeys((0, (regions - 1) % regions, 1 % regions)))
    geometry = (regions, tmpls, subs, offsets)
    in_specs = (
        P("region", ("tmpl", "sub"), "groups"),
        P("region", ("tmpl", "sub"), None, None),
        P("region", ("tmpl", "sub"), None),
        P("region", ("tmpl", "sub"), None),
        P("region", ("tmpl", "sub")),
        P("region", None, None),
        P("region", None),
    )
    return jax.shard_map(
        functools.partial(on_device, geometry),
        mesh=mesh,
        in_specs=in_specs,
        out_specs=P("region", ("tmpl", "sub"), "groups"),
        check_vma=False,
    )
```

time: 654 us -> 26.7 us (0.04)
  local copies, waits for them, and re-layouts: 573 us -> 3.22 us
  other arithmetic: 40.3 us -> 0 us
  Pallas kernels: 0 us -> 23.3 us
  blocking collectives: 15.7 us -> 0 us
  matrix products: 7.43 us -> 0 us
  loops' own time: 6.96 us -> 0 us
    gather x1156 -> x0, local copies, waits for them, and re-layouts: 570 us -> none
    cos x2 -> x0, other arithmetic: 25.3 us -> none  [the longest x1 12.7 us: inverse_table(): return jnp.concatenate([jnp.cos(phases), -jnp.sin(phases)], axis=0)]
    pallas_call x0 -> x2, Pallas kernels: none -> 23.3 us  [the longest x1 15.2 us: on_device(): pl.pallas_call(functools.partial(station_kernel, geometry), out_shape=(ja...]
    all_gather x1 -> x0, blocking collectives: 15.7 us -> none  [on_device(): region_rows = lax.all_gather(payload, ('tmpl', 'sub'), axis=0, tiled=True)]
    another operation x5 -> x0, other arithmetic: 11.9 us -> none
    dot_general x4 -> x0, matrix products: 7.43 us -> none  [the longest x1 3.34 us: on_device(): jnp.dot(waveforms[0], forward_table(NF, F0, BAND, NF), precision=lax.Prec...]
    another operation x1 -> x0, loops' own time: 6.96 us -> none  [block_scores(): lax.dynamic_slice_in_dim(series, offset, OUT)]
  transfers between devices with their start and end apart: 2 -> 0, of which waited for: 0 -> 0; matrix products, arithmetic and copies ran while one was open for 2% -> 0% of each run, Pallas kernels for 0% -> 0%
where the time goes in v1:
time: 26.7 us; the launch traced here: 26.5 us
  Pallas kernels  23.3 us (87%)
  local copies, waits for them, and re-layouts  3.22 us (12%)
    pallas_call x1, Pallas kernels, on_device(): pl.pallas_call(functools.partial(station_kernel, geometry), out_shape=(ja...  15.2 us
    pallas_call x1, Pallas kernels, on_device(): pl.pallas_call(functools.partial(match_kernel, geometry, chans, bmax), ou...  8.07 us
    unnamed x7, local copies, waits for them, and re-layouts  3.22 us

profile of v1, /device:TPU:0, one launch (start us, length us, event | category | flops | bytes accessed | tf_op | source)
XLA Modules:
  0.0 26.5 jit_solution(952220037373324274)
XLA Ops:
  0.0 0.0 copy-start
  0.0 0.0 copy-start.1
  0.0 1.8 %copy.20 = bf16[1,24,12,400]{3,2,1,0:T(8,128)(2,1)} copy(bf16[1,24,12,400]{3,1,2,0:T(8,128)(2,1)} %param.16) | data formatting | bytes 460800 | tf_op args[1]
  1.9 15.2 %stations.1 = (f32[16,32,128]{2,1,0:T(8,128)}, f32[384,768]{1,0:T(8,128)}, f32[384,1]{1,0:T(8,128)}) custom-call(f32[2,2048]{1,0:T(2,128)} %bitcast.11, s32[2,8]{1,0:T(2,128)} %bitcast.12, s32[1,2]{1,0:T(1,128)} %count_ref.1, bf16[24,12,400]{2,1,0:T(8,128)(2,1)} %bitcast.8, bf16[400,768]{1,0:T(8,128)(2,1)} %constant.16.clone.short_ref, ...), custom_call_target="tpu_custom_call" | custom-call | tf_op jit(solution)/shard_map/stations/pallas_call | solution.py:281
  17.1 0.0 copy-done
  17.1 0.7 %copy.17 = s32[1,24,12]{2,1,0:T(8,128)} copy(s32[1,24,12]{1,0,2:T(1,128)S(1)} %copy-done) | data formatting | bytes 2304 | tf_op args[2]
  17.8 0.0 copy-done.1
  17.8 0.7 %copy.18 = s32[1,24,12]{2,1,0:T(8,128)} copy(s32[1,24,12]{1,0,2:T(1,128)S(1)} %copy-done.1) | data formatting | bytes 2304 | tf_op args[3]
  18.5 8.1 %match.1 = f32[24,512]{1,0:T(8,128)} custom-call(f32[16,32,128]{2,1,0:T(8,128)} %get-tuple-element.8.recv_ref, f32[384,768]{1,0:T(8,128)} %get-tuple-element.9.tspec_ref, f32[384,1]{1,0:T(8,128)} %get-tuple-element.10.scale_ref, s32[24,12]{1,0:T(8,128)} %bitcast.9, s32[24,12]{1,0:T(8,128)} %bitcast.10, s32[1,24]{1,0:T(1,128)} %active_ref.1, ...), custom_call_target="tpu_custom_call" | custom-call | tf_op jit(solution)/shard_map/match/pallas_call | solution.py:304
Async XLA Ops:
  0.0 17.1 %copy-start = (s32[1,24,12]{1,0,2:T(1,128)S(1)}, s32[1,24,12]{1,0,2:T(1,128)}, u32[]{:S(2)}) copy-start(s32[1,24,12]{1,0,2:T(1,128)} %param.17) | copy-start | bytes 3460
  0.0 17.8 %copy-start.1 = (s32[1,24,12]{1,0,2:T(1,128)S(1)}, s32[1,24,12]{1,0,2:T(1,128)}, u32[]{:S(2)}) copy-start(s32[1,24,12]{1,0,2:T(1,128)} %param.18) | copy-start | bytes 3460

commit v2 on v1

--- a/solution.py
+++ b/solution.py
@@ -22,6 +22,8 @@
 STEPS = BAND // RES
 CHUNKS = (2 * BAND + LN) // LANES
 SPEC_CHUNKS = 2 * BAND // LANES
+STATION_INPUTS = 11
+MATCH_INPUTS = 7
 MESH = pl.DeviceIdType.MESH
 HIGH = lax.Precision.HIGHEST
 
@@ -73,11 +75,18 @@
     return [x.astype(np.float32) for x in (gather, spread, twiddle, fwd, inv, window)]
 
 
-def station_kernel(
-    geometry, wave_ref, border_ref, count_ref, tmpl_ref, short_ref, gather_ref, spread_ref,
-    twiddle_ref, fwd_ref, inv_ref, window_ref, recv_ref, tspec_ref, scale_ref,
-    pay_ref, rows_ref, spec_ref, pad_ref, send_sem, recv_sem,
-):
+def station_kernel(geometry, *refs):
+    count = STATION_INPUTS
+    hbm, (recv_ref, *out_hbm) = refs[:count], refs[count : count + 3]
+    (pay_ref, rows_ref, spec_ref), local = refs[count + 3 : count + 6], refs[count + 6 : 2 * count + 6]
+    tspec_ref, scale_ref, load_sem, send_sem, recv_sem = refs[2 * count + 6 :]
+    loads = [pltpu.make_async_copy(h, v, load_sem.at[i]) for i, (h, v) in enumerate(zip(hbm, local))]
+    for load in loads:
+        load.start()
+    (
+        wave_ref, gather_ref, twiddle_ref, fwd_ref, inv_ref, spread_ref, window_ref, border_ref,
+        count_ref, tmpl_ref, short_ref,
+    ) = local
     regions, tmpls, subs, offsets = geometry
     group = tmpls * subs
     region = lax.axis_index("region")
@@ -95,12 +104,16 @@
 
     chans = wave_ref.shape[0]
     half = RES * chans
+    loads[0].wait()
     for a in range(RES):
         rows_ref[chans * a : chans * (a + 1), :] = wave_ref[:, LANES * a : LANES * (a + 1)]
+    loads[1].wait()
     y = dot(gather_ref[...], rows_ref[...])
+    loads[2].wait()
     cos, sin = twiddle_ref[:half, :], twiddle_ref[half:, :]
     yr, yi = y[:half], y[half:]
     z = jnp.concatenate([yr * cos + yi * sin, yi * cos - yr * sin], axis=1)
+    loads[3].wait()
     x = dot(z, fwd_ref[...])
     for r in range(RES):
         piece = x[chans * r : chans * (r + 1), :]
@@ -108,16 +121,21 @@
         spec_ref[:, BAND + STEPS * r : BAND + STEPS * (r + 1)] = piece[:, STEPS : 2 * STEPS]
     for k in range(SPEC_CHUNKS):
         pay_ref[chans * k : chans * (k + 1), :] = spec_ref[:, LANES * k : LANES * (k + 1)]
+    loads[4].wait()
     v = dot(x, inv_ref[...])
     vr, vi = v[:, :LANES], v[:, LANES:]
     u = jnp.concatenate([vr * cos - vi * sin, vr * sin + vi * cos], axis=0)
+    loads[5].wait()
     filtered = dot(spread_ref[...], u)
     rows_ref[...] = filtered * filtered
     count = LN // LANES * chans
     near = lambda i: rows_ref[chans * i : chans * i + count, :]
     pieces = jnp.concatenate([near(0), near(1) + near(2), near(3), near(4)], axis=1)
     start = chans * SPEC_CHUNKS
+    loads[6].wait()
     pay_ref[start : start + count, :] = dot(pieces, window_ref[...])
+    loads[7].wait()
+    loads[8].wait()
     bmax = border_ref.shape[1]
     base = chans * CHUNKS
     pay_ref[base:, :] = jnp.zeros((pay_ref.shape[0] - base, LANES), jnp.float32)
@@ -138,18 +156,22 @@
         )
         copy.start()
         copies.append(copy)
-    recv_ref[pl.ds(place, 1)] = pay_ref[...][None]
-
-    templs, slots, _ = tmpl_ref.shape
-    pad_ref[...] = jnp.zeros_like(pad_ref)
-    for t in range(templs):
-        pad_ref[t, :slots, :] = tmpl_ref[t]
-    waves = pad_ref[...].reshape(templs * pad_ref.shape[1], K)
+    stores = [pltpu.make_async_copy(pay_ref, recv_ref.at[place], load_sem.at[0])]
+    stores[0].start()
+
+    loads[9].wait()
+    loads[10].wait()
+    waves = tmpl_ref[...]
     tspec_ref[...] = jnp.dot(waves, short_ref[...], preferred_element_type=jnp.float32)
     wide = waves.astype(jnp.float32)
     power = jnp.sum(wide * wide, axis=1, keepdims=True)
     scale_ref[...] = 2.0 / NF * lax.rsqrt(power + EPSILON)
-
+    for i, (v, h) in enumerate(zip((tspec_ref, scale_ref), out_hbm)):
+        stores.append(pltpu.make_async_copy(v, h, load_sem.at[i + 1]))
+        stores[-1].start()
+
+    for store in stores:
+        store.wait()
     for copy in copies:
         copy.wait_send()
     for block, step, peer, device in peers:
@@ -164,20 +186,24 @@
         ).wait_recv()
 
 
-def match_kernel(
-    geometry, chans, bmax, recv_ref, tspec_ref, scale_ref, ids_ref, move_ref, active_ref, lag_ref,
-    out_ref, table_ref, parts_ref, cross_ref, line_ref, sums_ref,
-):
+def match_kernel(geometry, chans, bmax, *refs):
+    count = MATCH_INPUTS
+    hbm, out_ref, local = refs[:count], refs[count], refs[count + 1 : 2 * count + 1]
+    table_ref, parts_ref, cross_ref, line_ref, sums_ref, load_sem = refs[2 * count + 1 :]
+    loads = [pltpu.make_async_copy(h, v, load_sem.at[i]) for i, (h, v) in enumerate(zip(hbm, local))]
+    for load in loads:
+        load.start()
+    recv_ref, ids_ref, tspec_ref, lag_ref, scale_ref, move_ref, active_ref = local
     regions, tmpls, subs, offsets = geometry
     group = tmpls * subs
     own = group * chans
     total = own * len(offsets)
     ext = own + 2 * bmax
-    templs, slots = ids_ref.shape
-    padded = tspec_ref.shape[0] // templs
-    wide = padded * templs
+    slots, _, templs = ids_ref.shape
+    wide = slots * templs
     bf16, f32 = jnp.bfloat16, jnp.float32
 
+    loads[0].wait()
     for d in range(group * len(offsets)):
         for k in range(CHUNKS):
             table_ref[chans * d : chans * (d + 1), LANES * k : LANES * (k + 1)] = recv_ref[
@@ -208,12 +234,16 @@
     left_pick = one((row == left * own + from_left[:, :bmax]) & (lane[:, :bmax] < left_count))
     right_pick = one((row == right * own + from_right[:, :bmax]) & (lane[:, :bmax] < right_count))
 
-    slot_row = lax.broadcasted_iota(jnp.int32, (wide, 1), 0)
-    spread = one(slot_row // padded == lax.broadcasted_iota(jnp.int32, (wide, templs), 1))
-    ids = ids_ref[...].astype(f32).astype(bf16)
-    ids = jnp.dot(spread, ids, preferred_element_type=f32)
-    mine = slot_row % padded == lax.broadcasted_iota(jnp.int32, (wide, slots), 1)
-    ids = jnp.sum(jnp.where(mine, ids, 0.0), axis=1, keepdims=True).astype(jnp.int32)
+    loads[1].wait()
+    square = (templs, templs)
+    same = lax.broadcasted_iota(jnp.int32, square, 0) == lax.broadcasted_iota(jnp.int32, square, 1)
+    ids = jnp.concatenate(
+        [
+            jnp.sum(jnp.where(same, ids_ref[j], 0), axis=1, keepdims=True, dtype=jnp.int32)
+            for j in range(slots)
+        ],
+        axis=0,
+    )
     contract = (((1,), (1,)), ((), ()))
     pick = lambda first, rows_pick: lax.dot_general(
         one(ids == first + lane[:, : rows_pick.shape[1]]), rows_pick, contract,
@@ -223,12 +253,15 @@
     chosen = chosen.astype(bf16)
 
     spec = jnp.dot(chosen, parts_ref[:, : 2 * BAND], preferred_element_type=f32)
+    loads[2].wait()
     xr, xi = spec[:, :BAND], spec[:, BAND:]
     wr, wi = tspec_ref[:, :BAND], tspec_ref[:, BAND:]
     cross_ref[:, :BAND] = (wr * xr + wi * xi).astype(bf16)
     cross_ref[:, BAND:] = (wr * xi - wi * xr).astype(bf16)
     unsent = (1.0 - jnp.sum(chosen.astype(f32), axis=1, keepdims=True) / 3.0) * EPSILON**-0.5
     step = 2 * LANES
+    loads[3].wait()
+    loads[4].wait()
     for c in range(0, LN, step):
         corr = jnp.dot(cross_ref[...], lag_ref[:, c : c + step], preferred_element_type=f32)
         inv = jnp.dot(
@@ -240,6 +273,8 @@
                 :, LANES * k : LANES * (k + 1)
             ]
 
+    loads[5].wait()
+    loads[6].wait()
     rows_out = OUT // LANES
     lane4 = lax.broadcasted_iota(jnp.int32, (rows_out, LANES), 1)
 
@@ -247,9 +282,9 @@
         total_score = jnp.zeros((rows_out, LANES), f32)
         used = active_ref[0, t]
         for j in range(slots):
-            move = move_ref[t, j]
+            move = move_ref[j, 0, t]
             q, s = move // LANES, move % LANES
-            start = (t * padded + j) * (LN // LANES) + q
+            start = (j * templs + t) * (LN // LANES) + q
             first = line_ref[pl.ds(start, rows_out), :]
             second = line_ref[pl.ds(start + 1, rows_out), :]
             joined = jnp.where(lane4 >= s, first, second)
@@ -271,13 +306,19 @@
     chans = waveforms.shape[1]
     bmax = border.shape[2]
     templs, slots = channel_ids.shape[1:]
-    padded = -(-slots // 16) * 16
-    wide = templs * padded
+    wide = slots * templs
+    by_slot = lambda x: jnp.transpose(x, (2, 0, 1))
     short_table, lag_table = wide_tables()
     pay_rows = -(-(chans * CHUNKS + 3) // 8) * 8
     vmem = pl.BlockSpec(memory_space=pltpu.VMEM)
-    smem = pl.BlockSpec(memory_space=pltpu.SMEM)
+    hbm = pl.BlockSpec(memory_space=pltpu.HBM)
     f32, bf16 = jnp.float32, jnp.bfloat16
+    gather, spread, twiddle, fwd, inv, window = small_tables(chans)
+    rows = jnp.swapaxes(templates[0], 0, 1).reshape(wide, K)
+    inputs = (
+        waveforms[0], gather, twiddle, fwd, inv, spread, window, border[0], border_count, rows,
+        short_table,
+    )
     recv, tspec, scale = pl.pallas_call(
         functools.partial(station_kernel, geometry),
         out_shape=(
@@ -285,36 +326,40 @@
             jax.ShapeDtypeStruct((wide, 2 * BAND), f32),
             jax.ShapeDtypeStruct((wide, 1), f32),
         ),
-        in_specs=[vmem] * 11,
-        out_specs=(vmem, vmem, vmem),
+        in_specs=[hbm] * STATION_INPUTS,
+        out_specs=(hbm, hbm, hbm),
         scratch_shapes=[
             pltpu.VMEM((pay_rows, LANES), f32),
             pltpu.VMEM((RES * chans, LANES), f32),
             pltpu.VMEM((chans, 2 * BAND), f32),
-            pltpu.VMEM((templs, padded, K), bf16),
+            *[pltpu.VMEM(x.shape, x.dtype) for x in inputs],
+            pltpu.VMEM((wide, 2 * BAND), f32),
+            pltpu.VMEM((wide, 1), f32),
+            pltpu.SemaphoreType.DMA((STATION_INPUTS,)),
             pltpu.SemaphoreType.DMA((devices,)),
             pltpu.SemaphoreType.DMA((devices,)),
         ],
         compiler_params=pltpu.CompilerParams(collective_id=0, has_side_effects=True),
         name="stations",
-    )(
-        waveforms[0], border[0], border_count, templates[0], short_table,
-        *small_tables(chans),
-    )
+    )(*inputs)
+    inputs = (recv, by_slot(channel_ids), tspec, lag_table, scale, by_slot(moveouts), active)
+    spaces = [pltpu.VMEM] * 5 + [pltpu.SMEM] * 2
     scores = pl.pallas_call(
         functools.partial(match_kernel, geometry, chans, bmax),
         out_shape=jax.ShapeDtypeStruct((templs, OUT), f32),
-        in_specs=[vmem, vmem, vmem, vmem, smem, smem, vmem],
+        in_specs=[hbm] * MATCH_INPUTS,
         out_specs=vmem,
         scratch_shapes=[
+            *[space(x.shape, x.dtype) for space, x in zip(spaces, inputs)],
             pltpu.VMEM((chans * devices, CHUNKS * LANES), f32),
             pltpu.VMEM((3 * chans * devices, CHUNKS * LANES), bf16),
             pltpu.VMEM((wide, 2 * BAND), bf16),
             pltpu.VMEM((wide * (LN // LANES), LANES), f32),
             pltpu.VMEM((templs * (OUT // LANES), LANES), f32),
+            pltpu.SemaphoreType.DMA((MATCH_INPUTS,)),
         ],
         name="match",
-    )(recv, tspec, scale, channel_ids[0], moveouts[0], active, lag_table)
+    )(*inputs)
     return scores[None]
 
 

time: 26.7 us -> 21 us (0.79)
  local copies, waits for them, and re-layouts: 3.22 us -> 0 us
  Pallas kernels: 23.3 us -> 20.8 us
    unnamed x7 -> x0, local copies, waits for them, and re-layouts: 3.22 us -> none
    pallas_call x1, Pallas kernels: 15.2 us -> 13.3 us  [on_device(): pl.pallas_call(functools.partial(station_kernel, geometry), out_shape=(ja...]
    pallas_call x1, Pallas kernels: 8.07 us -> 7.5 us  [on_device(): pl.pallas_call(functools.partial(match_kernel, geometry, chans, bmax), ou...]
where the time goes in v2:
time: 21 us; the launch traced here: 20.8 us
  Pallas kernels  20.8 us (99%)
    pallas_call x1, Pallas kernels, on_device(): pl.pallas_call(functools.partial(station_kernel, geometry), out_shape=(ja...  13.3 us
    pallas_call x1, Pallas kernels, on_device(): pl.pallas_call(functools.partial(match_kernel, geometry, chans, bmax), ou...  7.5 us

profile of v2, /device:TPU:0, one launch (start us, length us, event | category | flops | bytes accessed | tf_op | source)
XLA Modules:
  0.0 20.8 jit_solution(9147743351908247239)
XLA Ops:
  0.0 13.3 %stations.1 = (f32[16,32,128]{2,1,0:T(8,128)}, f32[288,768]{1,0:T(8,128)}, f32[288,1]{1,0:T(8,128)}) custom-call(f32[2,2048]{1,0:T(2,128)} %bitcast.11, f32[64,32]{1,0:T(8,128)} %constant.16.clone.refs_1_, f32[64,128]{1,0:T(8,128)} %constant.17.clone.refs_2_, f32[256,128]{1,0:T(8,128)} %constant.18.clone.refs_3_, f32[128,256]{1,0:T(8,128)} %constant.19.clone.refs_4_, ...), custom_call_target="tpu_custom_call" | custom-call | tf_op jit(solution)/shard_map/stations/pallas_call | solution.py:322
  13.3 7.5 %match.1 = f32[24,512]{1,0:T(8,128)} custom-call(f32[16,32,128]{2,1,0:T(8,128)} %get-tuple-element.8.refs_0_, s32[12,1,24]{2,1,0:T(1,128)} %bitcast.12, f32[288,768]{1,0:T(8,128)} %get-tuple-element.9.refs_2_, bf16[768,1024]{1,0:T(8,128)(2,1)} %constant.23.clone.refs_3_, f32[288,1]{1,0:T(8,128)} %get-tuple-element.10.refs_4_, s32[12,1,24]{2,1,0:T(1,128)} %bitcast.13, ...), custom_call_target="tpu_custom_call" | custom-call | tf_op jit(solution)/shard_map/match/pallas_call | solution.py:347

commit v3 on v2

--- a/solution.py
+++ b/solution.py
@@ -91,15 +91,27 @@
     group = tmpls * subs
     region = lax.axis_index("region")
     place = lax.axis_index("tmpl") * subs + lax.axis_index("sub")
+    tmpl, sub = lax.axis_index("tmpl"), lax.axis_index("sub")
     peers = []
     for block, offset in enumerate(offsets):
         there = lax.rem(region + (regions - offset) % regions, regions)
-        for step in range(1 if offset == 0 else 0, group):
-            peer = lax.rem(place + step, group)
-            device = {"region": there, "tmpl": peer // subs, "sub": lax.rem(peer, subs)}
-            peers.append((block, step, peer, device))
+        for step in range(1 if offset == 0 else 0, tmpls):
+            peer = lax.rem(tmpl + step, tmpls)
+            peers.append((block, peer * subs + sub, {"region": there, "tmpl": peer, "sub": sub}))
+    mates = [lax.rem(sub + step, subs) for step in range(1, subs)]
+
+    def copy_to(slot, source, device, lane):
+        return pltpu.make_async_remote_copy(
+            src_ref=source,
+            dst_ref=recv_ref.at[slot],
+            send_sem=send_sem.at[lane],
+            recv_sem=recv_sem.at[slot],
+            device_id=device,
+            device_id_type=MESH,
+        )
+
     barrier = pltpu.get_barrier_semaphore()
-    for _, _, _, device in peers:
+    for device in [device for _, _, device in peers] + [{"sub": mate} for mate in mates]:
         pl.semaphore_signal(barrier, inc=1, device_id=device, device_id_type=MESH)
 
     chans = wave_ref.shape[0]
@@ -143,19 +155,17 @@
     pay_ref[base + 1 : base + 2, :bmax] = border_ref[0:1, :].astype(jnp.float32)
     pay_ref[base + 2 : base + 3, :2] = count_ref[...].astype(jnp.float32)
 
-    pl.semaphore_wait(barrier, len(peers))
+    pl.semaphore_wait(barrier, len(peers) + len(mates))
     copies = []
-    for block, step, peer, device in peers:
-        copy = pltpu.make_async_remote_copy(
-            src_ref=pay_ref,
-            dst_ref=recv_ref.at[block * group + place],
-            send_sem=send_sem.at[block * group + step],
-            recv_sem=recv_sem.at[block * group + place],
-            device_id=device,
-            device_id_type=MESH,
-        )
-        copy.start()
-        copies.append(copy)
+
+    def send(slot, source, device):
+        copies.append(copy_to(slot, source, device, len(copies)))
+        copies[-1].start()
+
+    for block, peer, device in reversed(peers):
+        send(block * group + place, pay_ref, device)
+    for mate in mates:
+        send(place, pay_ref, {"sub": mate})
     stores = [pltpu.make_async_copy(pay_ref, recv_ref.at[place], load_sem.at[0])]
     stores[0].start()
 
@@ -172,18 +182,18 @@
 
     for store in stores:
         store.wait()
+    for block, peer, device in peers:
+        slot = block * group + peer
+        copy_to(slot, pay_ref, device, 0).wait_recv()
+        for mate in mates:
+            send(slot, recv_ref.at[slot], {"sub": mate})
+    for mate in mates:
+        for block in range(len(offsets)):
+            for step in range(tmpls):
+                slot = block * group + lax.rem(tmpl + step, tmpls) * subs + mate
+                copy_to(slot, pay_ref, {"sub": mate}, 0).wait_recv()
     for copy in copies:
         copy.wait_send()
-    for block, step, peer, device in peers:
-        slot = block * group + peer
-        pltpu.make_async_remote_copy(
-            src_ref=pay_ref,
-            dst_ref=recv_ref.at[slot],
-            send_sem=send_sem.at[block * group + step],
-            recv_sem=recv_sem.at[slot],
-            device_id=device,
-            device_id_type=MESH,
-        ).wait_recv()
 
 
 def match_kernel(geometry, chans, bmax, *refs):
@@ -283,17 +293,17 @@
         used = active_ref[0, t]
         for j in range(slots):
             move = move_ref[j, 0, t]
-            q, s = move // LANES, move % LANES
+            q, s = move >> 7, move & (LANES - 1)
             start = (j * templs + t) * (LN // LANES) + q
             first = line_ref[pl.ds(start, rows_out), :]
             second = line_ref[pl.ds(start + 1, rows_out), :]
             joined = jnp.where(lane4 >= s, first, second)
-            turned = pltpu.roll(joined, (LANES - s) % LANES, 1)
+            turned = pltpu.roll(joined, (LANES - s) & (LANES - 1), 1)
             total_score += turned * jnp.where(j < used, 1.0, 0.0)
         sums_ref[pl.ds(t * rows_out, rows_out), :] = total_score
         return carry
 
-    lax.fori_loop(0, templs, one_template, 0)
+    lax.fori_loop(0, templs, one_template, 0, unroll=8)
     for a in range(rows_out):
         out_ref[:, LANES * a : LANES * (a + 1)] = sums_ref[pl.ds(a, templs, stride=rows_out), :]
 

time: 21 us -> 16.7 us (0.80)
  Pallas kernels: 20.8 us -> 16.5 us
    pallas_call x1, Pallas kernels: 7.5 us -> 4.63 us  [on_device(): pl.pallas_call(functools.partial(match_kernel, geometry, chans, bmax), ou...]
    pallas_call x1, Pallas kernels: 13.3 us -> 11.9 us  [on_device(): pl.pallas_call(functools.partial(station_kernel, geometry), out_shape=(ja...]
where the time goes in v3:
time: 16.7 us; the launch traced here: 16.5 us
  Pallas kernels  16.5 us (99%)
    pallas_call x1, Pallas kernels, on_device(): pl.pallas_call(functools.partial(station_kernel, geometry), out_shape=(ja...  11.9 us
    pallas_call x1, Pallas kernels, on_device(): pl.pallas_call(functools.partial(match_kernel, geometry, chans, bmax), ou...  4.63 us

profile of v3, /device:TPU:0, one launch (start us, length us, event | category | flops | bytes accessed | tf_op | source)
XLA Modules:
  0.0 16.5 jit_solution(8660898599180827433)
XLA Ops:
  0.0 11.9 %stations.1 = (f32[16,32,128]{2,1,0:T(8,128)}, f32[288,768]{1,0:T(8,128)}, f32[288,1]{1,0:T(8,128)}) custom-call(f32[2,2048]{1,0:T(2,128)} %bitcast.11, f32[64,32]{1,0:T(8,128)} %constant.16.clone.refs_1_, f32[64,128]{1,0:T(8,128)} %constant.17.clone.refs_2_, f32[256,128]{1,0:T(8,128)} %constant.18.clone.refs_3_, f32[128,256]{1,0:T(8,128)} %constant.19.clone.refs_4_, ...), custom_call_target="tpu_custom_call" | custom-call | tf_op jit(solution)/shard_map/stations/pallas_call | solution.py:332
  11.9 4.6 %match.1 = f32[24,512]{1,0:T(8,128)} custom-call(f32[16,32,128]{2,1,0:T(8,128)} %get-tuple-element.8.refs_0_, s32[12,1,24]{2,1,0:T(1,128)} %bitcast.12, f32[288,768]{1,0:T(8,128)} %get-tuple-element.9.refs_2_, bf16[768,1024]{1,0:T(8,128)(2,1)} %constant.23.clone.refs_3_, f32[288,1]{1,0:T(8,128)} %get-tuple-element.10.refs_4_, s32[12,1,24]{2,1,0:T(1,128)} %bitcast.13, ...), custom_call_target="tpu_custom_call" | custom-call | tf_op jit(solution)/shard_map/match/pallas_call | solution.py:357

commit v4 on v3

--- a/solution.py
+++ b/solution.py
@@ -72,7 +72,8 @@
         place = LANES * i + b[:, None] - b[None, :]
         rows.append((place >= 0) & (place < K))
     window = np.concatenate(rows, axis=0)
-    return [x.astype(np.float32) for x in (gather, spread, twiddle, fwd, inv, window)]
+    tables = [x.astype(np.float32) for x in (gather, spread, twiddle, fwd, inv)]
+    return tables + [window.astype(np.float32).astype(ml_dtypes.bfloat16)]
 
 
 def station_kernel(geometry, *refs):
@@ -145,7 +146,14 @@
     pieces = jnp.concatenate([near(0), near(1) + near(2), near(3), near(4)], axis=1)
     start = chans * SPEC_CHUNKS
     loads[6].wait()
-    pay_ref[start : start + count, :] = dot(pieces, window_ref[...])
+    high = pieces.astype(jnp.bfloat16)
+    rest = pieces - high.astype(jnp.float32)
+    middle = rest.astype(jnp.bfloat16)
+    low = (rest - middle.astype(jnp.float32)).astype(jnp.bfloat16)
+    stacked = jnp.concatenate([high, middle, low], axis=0)
+    sums = jnp.dot(stacked, window_ref[...], preferred_element_type=jnp.float32)
+    energy = sums[:count] + (sums[count : 2 * count] + sums[2 * count :])
+    pay_ref[start : start + count, :] = energy
     loads[7].wait()
     loads[8].wait()
     bmax = border_ref.shape[1]

time: 16.7 us -> 16.6 us (level)
  no operation moved by 1% of the time
where the time goes in v4:
time: 16.6 us; the launch traced here: 16.4 us
  Pallas kernels  16.4 us (99%)
    pallas_call x1, Pallas kernels, on_device(): pl.pallas_call(functools.partial(station_kernel, geometry), out_shape=(ja...  11.8 us
    pallas_call x1, Pallas kernels, on_device(): pl.pallas_call(functools.partial(match_kernel, geometry, chans, bmax), ou...  4.63 us

profile of v4, /device:TPU:0, one launch (start us, length us, event | category | flops | bytes accessed | tf_op | source)
XLA Modules:
  0.0 16.4 jit_solution(15377452854221054411)
XLA Ops:
  0.0 11.8 %stations.1 = (f32[16,32,128]{2,1,0:T(8,128)}, f32[288,768]{1,0:T(8,128)}, f32[288,1]{1,0:T(8,128)}) custom-call(f32[2,2048]{1,0:T(2,128)} %bitcast.11, f32[64,32]{1,0:T(8,128)} %constant.16.clone.refs_1_, f32[64,128]{1,0:T(8,128)} %constant.17.clone.refs_2_, f32[256,128]{1,0:T(8,128)} %constant.18.clone.refs_3_, f32[128,256]{1,0:T(8,128)} %constant.19.clone.refs_4_, ...), custom_call_target="tpu_custom_call" | custom-call | tf_op jit(solution)/shard_map/stations/pallas_call | solution.py:340
  11.8 4.6 %match.1 = f32[24,512]{1,0:T(8,128)} custom-call(f32[16,32,128]{2,1,0:T(8,128)} %get-tuple-element.8.refs_0_, s32[12,1,24]{2,1,0:T(1,128)} %bitcast.12, f32[288,768]{1,0:T(8,128)} %get-tuple-element.9.refs_2_, bf16[768,1024]{1,0:T(8,128)(2,1)} %constant.23.clone.refs_3_, f32[288,1]{1,0:T(8,128)} %get-tuple-element.10.refs_4_, s32[12,1,24]{2,1,0:T(1,128)} %bitcast.13, ...), custom_call_target="tpu_custom_call" | custom-call | tf_op jit(solution)/shard_map/match/pallas_call | solution.py:365
